TPU v7x, 32 devices: a whole 2x2x4 slice. The times are simulated.
32 devices in a mesh: groups: 2 (over x), ind: 16 (over z, y, core).
Axes of the slice: x: 2, y: 2, z: 4, core: 2. Of those that a mesh axis runs over, the one named last changes fastest.
Arguments:
- genotype: bfloat16 [12288, 16384], P(('groups', 'ind')), parts along dimension 0, may hold values from -4 to 4
- residual: bfloat16 [12288, 256], P(('groups', 'ind')), parts along dimension 0, may hold values from -4 to 4
- labels: int32 [12288, 256], P(('groups', 'ind')), parts along dimension 0, may hold values 0 or 1
- incl_old: float32 [32768, 256], P(('groups', 'ind')), parts along dimension 0, may hold values from 0.02 to 0.98
- mean_old: float32 [32768, 256], P(('groups', 'ind')), parts along dimension 0, may hold values from -0.078125 to 0.078125
- prior_logit: float32 [256], replicated, may hold values from -4 to 0
- slab_scale: float32 [256], replicated, may hold values from 0.25 to 8
- offset: float32 [256], replicated, may hold values from -2 to 1
Outputs:
- incl_new: float32 [32768, 256], P(('groups', 'ind')), parts along dimension 0
- mean_new: float32 [32768, 256], P(('groups', 'ind')), parts along dimension 0
- resid_new: float32 [12288, 256], P(('groups', 'ind')), parts along dimension 0
There are 2 independent parts, one for each index of `groups`. A program takes and returns all parts, laid end to end along the dimension named above; an argument that names none is the same for every part. Nothing has to cross between parts.
All inputs are finite; a program needn't handle non-finite values. No bound on the sum of `labels` on one device may be relied on, other than what follows from the above.
Results may differ from a plain program's by a relative error of at most 0.00062.
Values may be sent and summed in bfloat16 or wider, within the bound.
A program may use at most 128 MiB of HBM per device.

v0:
```python
import jax
import jax.numpy as jnp
from jax import lax
from jax.sharding import PartitionSpec as P


def update(corr, incl_part, mean_part, prior_part, scale_part, total):
    stat = corr / total + incl_part * mean_part
    shrink = scale_part / (1.0 + scale_part)
    mean_new = stat * shrink
    logit = prior_part - 0.5 * jnp.log1p(scale_part) + 0.5 * total * shrink * stat * stat
    incl_new = 0.5 * incl_part + 0.5 * jax.nn.sigmoid(logit)
    effect = (incl_new * mean_new).astype(jnp.bfloat16)
    return (incl_new, mean_new, effect)


def on_device(genotype, residual, labels, incl_old, mean_old, prior_logit, slab_scale, offset):
    total = genotype.shape[0] * lax.axis_size("ind")
    columns = genotype
    corr = lax.psum_scatter(
        lax.dot_general(
            columns, residual, (((0,), (0,)), ((), ())), preferred_element_type=jnp.float32
        ),
        "ind",
        scatter_dimension=0,
        tiled=True,
    )
    incl_new, mean_new, effect = update(corr, incl_old, mean_old, prior_logit, slab_scale, total)
    columns = genotype
    eta = jnp.dot(
        columns,
        lax.all_gather(effect, "ind", axis=0, tiled=True),
        preferred_element_type=jnp.float32,
    )
    eta = eta + offset
    resid_new = 4.0 * (labels.astype(jnp.float32) - jax.nn.sigmoid(eta))
    return (incl_new, mean_new, resid_new)


def solution(mesh):
    placed = (
        P(("groups", "ind"), None),
        P(("groups", "ind"), None),
        P(("groups", "ind"), None),
        P(("groups", "ind"), None),
        P(("groups", "ind"), None),
        P(),
        P(),
        P(),
    )
    return jax.shard_map(
        on_device,
        mesh=mesh,
        in_specs=placed,
        out_specs=(
            P(("groups", "ind"), None),
            P(("groups", "ind"), None),
            P(("groups", "ind"), None),
        ),
        check_vma=False,
    )
```

profile of v0, /device:TPU:0, one launch (start us, length us, event | category | flops | bytes accessed | tf_op | source)
XLA Modules:
  0.0 301.3 jit_solution(4936477498398542598)
XLA Ops:
  7.2 0.0 copy-start
  7.2 0.0 reduce-scatter.2.cloned.1.call-start
  7.2 0.9 copy-done
  8.1 14.9 %fusion.15 = f32[16384,256]{1,0:T(8,128)} fusion(bf16[384,16384]{1,0:T(8,128)(2,1)} %param.8, bf16[384,256]{1,0:T(8,128)(2,1)S(1)} %copy-done), kind=kOutput, calls=%fused_computation.22 | convolution fusion | flops 3221225472 | bytes 29556736 | tf_op jit(solution)/shard_map/dot_general | solution.py:21
  23.0 0.0 copy-start.4
  23.0 0.0 copy-start.5
  23.0 0.0 copy-start.1
  23.0 0.0 copy-start.2
  23.0 0.0 copy-start.3
  23.0 0.0 copy-start.6
  23.0 0.0 reduce-scatter.2.cloned.1.call-update
  23.0 0.0 all-gather.2.cloned.1.call-start
  23.1 0.6 copy-done.4
  23.7 0.0 copy-done.5
  23.7 179.6 %reduce-scatter.2.cloned.1.call-done = f32[1024,256]{1,0:T(8,128)} async-done(((f32[16384,256]{1,0:T(8,128)}), f32[1024,256]{1,0:T(8,128)}) %reduce-scatter.2.cloned.1.call-update) | async-done | bytes 1048592 | tf_op jit(solution)/shard_map/reduce_scatter | solution.py:20
  203.3 0.0 copy-done.1
  203.3 0.0 copy-done.2
  203.3 3.0 %multiply_convert_fusion = (bf16[1024,256]{1,0:T(8,128)(2,1)}, f32[1024,256]{1,0:T(8,128)}, f32[1024,256]{1,0:T(8,128)}) fusion(f32[256]{0:T(256)S(1)} %get-tuple-element.10, f32[1024,256]{1,0:T(8,128)S(1)} %copy-done.1, f32[1024,256]{1,0:T(8,128)S(1)} %copy-done.2, f32[1024,256]{1,0:T(8,128)} %reduce-scatter.2.cloned.1.call-done, ...), kind=kLoop, calls=%fused_computation.15 | loop fusion | flops 3670016 | bytes 5770240 | tf_op jit(solution)/shard_map/convert_element_type | solution.py:13
  206.3 0.0 all-gather.2.cloned.1.call-update
  206.3 0.0 copy-done.3
  206.3 0.2 copy.11
  206.5 73.4 %all-gather.2.cloned.1.call-done = bf16[16384,256]{1,0:T(8,128)(2,1)} async-done(((bf16[1024,256]{1,0:T(8,128)(2,1)}), bf16[16384,256]{1,0:T(8,128)(2,1)}) %all-gather.2.cloned.1.call-update) | async-done | bytes 8388624 | tf_op jit(solution)/shard_map/all_gather | solution.py:32
  279.9 0.0 copy-done.6
  279.9 13.6 %fusion.6 = f32[384,256]{0,1:T(8,128)S(1)} fusion(bf16[16384,256]{1,0:T(8,128)(2,1)} %all-gather.2.cloned.1.call-done, bf16[384,16384]{1,0:T(8,128)(2,1)} %param.8, s32[384,256]{0,1:T(8,128)S(1)} %copy.11, f32[256]{0:T(256)S(1)} %copy-done.6), kind=kOutput, calls=%fused_computation.8 | convolution fusion | flops 3221913600 | bytes 21758976 | tf_op jit(solution)/shard_map/dot_general | solution.py:30
  293.5 0.9 copy.12
  (1 shorter events, 0.0 us)
Async XLA Ops:
  7.2 0.9 copy-start
  7.2 196.1 %reduce-scatter.2.cloned.1.call-start = ((), (), s32[]{:S(2)}) async-start(), calls=%async_computation.1 | async-start | bytes 17825792 | tf_op jit(solution)/shard_map/reduce_scatter | solution.py:20
  23.0 0.7 copy-start.4
  23.0 0.7 copy-start.5
  23.0 180.3 %copy-start.1 = (f32[1024,256]{1,0:T(8,128)S(1)}, f32[1024,256]{1,0:T(8,128)}, u32[]{:S(2)}) copy-start(f32[1024,256]{1,0:T(8,128)} %param.11) | copy-start | bytes 3145732
  23.0 180.3 %copy-start.2 = (f32[1024,256]{1,0:T(8,128)S(1)}, f32[1024,256]{1,0:T(8,128)}, u32[]{:S(2)}) copy-start(f32[1024,256]{1,0:T(8,128)} %param.12) | copy-start | bytes 3145732
  23.0 183.3 %copy-start.3 = (s32[384,256]{1,0:T(8,128)S(1)}, s32[384,256]{1,0:T(8,128)}, u32[]{:S(2)}) copy-start(s32[384,256]{1,0:T(8,128)} %param.10) | copy-start | bytes 1179652
  23.0 256.9 %copy-start.6 = (f32[256]{0:T(256)S(1)}, f32[256]{0:T(256)}, u32[]{:S(2)}) copy-start(f32[256]{0:T(256)} %param.15) | copy-start | bytes 3076
  23.0 256.8 %all-gather.2.cloned.1.call-start = ((), (), s32[]{:S(2)}) async-start(), calls=%async_computation.2 | async-start | bytes 8912896 | tf_op jit(solution)/shard_map/all_gather | solution.py:32
Sparse Core Ops, SparseCore 0:
  23.2 180.0 reduce-scatter.1
  206.4 73.3 all-gather.1
where the time goes:
time: 302 us; the launch traced here: 301 us
  waiting for transfers between devices  253 us (84%)
  matrix products  28.5 us (9%)
  between operations  14.1 us (5%)
  other arithmetic  3.04 us (1%)
    reduce_scatter x1, waiting for transfers between devices, on_device(): lax.psum_scatter(lax.dot_general(columns, residual, (((0,), (0,)), ((), (...  180 us
    all_gather x1, waiting for transfers between devices, on_device(): lax.all_gather(effect, 'ind', axis=0, tiled=True)  73.4 us
    dot_general x1, matrix products, on_device(): lax.dot_general(columns, residual, (((0,), (0,)), ((), ())), preferred_el...  14.9 us
    dot_general x1, matrix products, on_device(): jnp.dot(columns, lax.all_gather(effect, 'ind', axis=0, tiled=True), prefe...  13.6 us
  transfers between devices with their start and end apart: 2, of which 2 were waited for; matrix products, arithmetic and copies ran while one was open for 0% of the time, Pallas kernels for 0%

commit v1 on v0

v1 whole, which is shorter than its diff:
```python
import functools
import math

import jax
import jax.numpy as jnp
from jax import lax
from jax.experimental import pallas as pl
from jax.experimental.pallas import tpu as pltpu
from jax.sharding import PartitionSpec as P

LARGEST_TERM = 64.0


def sweep_kernel(
    n, chunks,
    geno_hbm, resid_ref, labels_hbm, incl_hbm, mean_hbm, prior_ref, scale_ref, offset_ref,
    incl_out, mean_out, resid_out,
    geno, labels, incl, mean, core_out, core_in, pair_out, pair_in, own, line_out, line_in, eff, eta,
    geno_sem, in_sem, core_ss, core_rs, pair_ss, pair_rs, line_ss, line_rs,
    gz_ss, gz_rs, gy_ss, gy_rs, gc_ss, gc_rs,
):
    length = n // 4
    owned = incl.shape[0]
    rows = owned // chunks
    people = geno.shape[0]
    total = float(people * n)
    coding = 32760.0 / math.log(1.0 + LARGEST_TERM * total)
    me = lax.axis_index("ind")
    z = me // 4
    y = (me // 2) % 2
    c = me % 2

    def at(zz, yy, cc):
        return zz * 4 + yy * 2 + cc

    core_dev = {"ind": at(z, y, 1 - c)}
    pair_dev = {"ind": at(z, 1 - y, c)}
    up_dev = {"ind": at(lax.rem(z + 1, length), y, c)}
    down_dev = {"ind": at(lax.rem(z + length - 1, length), y, c)}
    has_up = z < length - 1
    has_down = z > 0

    def remote(src, dst, ss, rs, dev):
        return pltpu.make_async_remote_copy(
            src_ref=src, dst_ref=dst, send_sem=ss, recv_sem=rs,
            device_id=dev, device_id_type=pl.DeviceIdType.MESH,
        )

    def encode(x):
        code = (jnp.log(1.0 + jnp.abs(x)) * coding + 0.5).astype(jnp.int32)
        return jnp.where(x < 0.0, -code, code).astype(jnp.int16)

    def decode(code):
        level = code.astype(jnp.int32).astype(jnp.float32)
        size = jnp.exp(jnp.abs(level) * (1.0 / coding)) - 1.0
        return jnp.where(level < 0.0, -size, size)

    def cols(s, o):
        return pl.ds(pl.multiple_of(o * owned + s * rows, 128), rows)

    def load(s, o):
        return pltpu.make_async_copy(
            geno_hbm.at[:, cols(s, o)], geno.at[:, cols(s, o)], geno_sem.at[s, o]
        )

    def for_z(body):
        lax.fori_loop(0, length, lambda i, _: (body(i), 0)[1], 0)

    def loop(count, body):
        lax.fori_loop(0, count, lambda i, _: (body(i), 0)[1], 0)

    owners = ((1 - y, 1 - c), (y, 1 - c), (y, c), (1 - y, c))

    def load_chunk(s):
        for yy, cc in owners:
            for_z(lambda i: load(s, at(i, yy, cc)).start())

    loop(chunks, load_chunk)
    small = [
        pltpu.make_async_copy(labels_hbm, labels, in_sem.at[0]),
        pltpu.make_async_copy(incl_hbm, incl, in_sem.at[1]),
        pltpu.make_async_copy(mean_hbm, mean, in_sem.at[2]),
    ]
    for copy in small:
        copy.start()

    barrier = pltpu.get_barrier_semaphore()
    pl.semaphore_signal(barrier, inc=1, device_id=core_dev, device_id_type=pl.DeviceIdType.MESH)
    pl.semaphore_signal(barrier, inc=1, device_id=pair_dev, device_id_type=pl.DeviceIdType.MESH)

    @pl.when(has_up)
    def _():
        pl.semaphore_signal(barrier, inc=1, device_id=up_dev, device_id_type=pl.DeviceIdType.MESH)

    @pl.when(has_down)
    def _():
        pl.semaphore_signal(barrier, inc=1, device_id=down_dev, device_id_type=pl.DeviceIdType.MESH)

    pl.semaphore_wait(barrier, 2 + has_up.astype(jnp.int32) + has_down.astype(jnp.int32))

    def product(s, o):
        load(s, o).wait()
        return lax.dot_general(
            geno[:, cols(s, o)], resid_ref[...], (((0,), (0,)), ((), ())),
            preferred_element_type=jnp.float32,
        )

    def core_copy(s, h):
        return remote(core_out.at[s, h], core_in.at[s, h], core_ss.at[s, h], core_rs.at[s, h], core_dev)

    def pair_copy(s):
        return remote(pair_out.at[s], pair_in.at[s], pair_ss.at[s], pair_rs.at[s], pair_dev)

    def line_copy(s, t, d):
        return remote(
            line_out.at[s, t, d], line_in.at[s, t, d], line_ss.at[s, t, d], line_rs.at[s, t, d],
            up_dev if d == 0 else down_dev,
        )

    def first(s):
        for h in range(2):
            yy, cc = owners[h]

            def part(i):
                core_out[s, h, i] = product(s, at(i, yy, cc))

            for_z(part)
            core_copy(s, h).start()

        def keep(i):
            own[s, i] = product(s, at(i, y, c))

        for_z(keep)
        core_copy(s, 0).wait_recv()

        def pass_on(i):
            pair_out[s, i] = encode(product(s, at(i, 1 - y, c)) + core_in[s, 0, i])

        for_z(pass_on)
        pair_copy(s).start()

    loop(chunks, first)
    for copy in small:
        copy.wait()
    eta[...] = jnp.zeros_like(eta)

    scale = scale_ref[...]
    shrink = scale / (1.0 + scale)
    bias = prior_ref[...] - 0.5 * jnp.log1p(scale)
    curve = 0.5 * total * shrink

    def along(s, t):
        @pl.when(t == 0)
        def _():
            core_copy(s, 1).wait_recv()
            pair_copy(s).wait_recv()

            def add(i):
                own[s, i] = own[s, i] + core_in[s, 1, i] + decode(pair_in[s, i])

            for_z(add)

        for d in range(2):
            place = z if d == 0 else length - 1 - z
            block = length - 1 - t + z if d == 0 else t - (length - 1 - z)

            @pl.when((place <= t) & (place < length - 1))
            def _():
                @pl.when(place == 0)
                def _():
                    line_out[s, t, d] = encode(own[s, block])

                @pl.when(place > 0)
                def _():
                    line_copy(s, t - 1, d).wait_recv()
                    line_out[s, t, d] = encode(own[s, block] + decode(line_in[s, t - 1, d]))

                line_copy(s, t, d).start()

    def gz_copy(s, u, d):
        o = at(z - u if d == 0 else z + u, y, c)
        return remote(
            eff.at[s, o], eff.at[s, o], gz_ss.at[s, u, d], gz_rs.at[s, u, d], up_dev if d == 0 else down_dev
        )

    def gz_landed(s, u, d):
        o = at(z - 1 - u if d == 0 else z + 1 + u, y, c)
        return remote(
            eff.at[s, o], eff.at[s, o], gz_ss.at[s, u, d], gz_rs.at[s, u, d], up_dev if d == 0 else down_dev
        )

    def gy_copy(s, i, yy):
        o = at(i, yy, c)
        return remote(eff.at[s, o], eff.at[s, o], gy_ss.at[s, i], gy_rs.at[s, i], pair_dev)

    def gc_copy(s, i, yy, cc):
        o = at(i, yy, cc)
        return remote(eff.at[s, o], eff.at[s, o], gc_ss.at[s, yy, i], gc_rs.at[s, yy, i], core_dev)

    def use(s, o):
        eta[...] += jnp.dot(geno[:, cols(s, o)], eff[s, o], preferred_element_type=jnp.float32)

    def finish(s):
        for d in range(2):
            @pl.when(has_down if d == 0 else has_up)
            def _():
                line_copy(s, length - 2, d).wait_recv()
                own[s, z] = own[s, z] + decode(line_in[s, length - 2, d])

        here = pl.ds(pl.multiple_of(s * rows, 8), rows)
        before = incl[here, :]
        stat = own[s, z] / total + before * mean[here, :]
        mean_new = stat * shrink
        incl_new = 0.5 * before + 0.5 * jax.nn.sigmoid(bias + curve * stat * stat)
        mean_out[here, :] = mean_new
        incl_out[here, :] = incl_new
        eff[s, me] = (incl_new * mean_new).astype(jnp.bfloat16)

        @pl.when(has_up)
        def _():
            gz_copy(s, 0, 0).start()

        @pl.when(has_down)
        def _():
            gz_copy(s, 0, 1).start()

        gy_copy(s, z, y).start()
        gc_copy(s, z, y, c).start()
        use(s, me)

    def spread(s, u):
        for d in range(2):
            source = z - u if d == 0 else z + u

            @pl.when((source >= 0) & (source < length))
            def _():
                gz_landed(s, u - 1, d).wait_recv()

                @pl.when(has_up if d == 0 else has_down)
                def _():
                    gz_copy(s, u, d).start()

                gy_copy(s, source, y).start()
                gc_copy(s, source, y, c).start()
                use(s, at(source, y, c))

    def wave(w):
        def gather_step(k):
            u = length - 1 - k
            s = w - (length - 1) - u

            @pl.when((s >= 0) & (s < chunks))
            def _():
                spread(s, u)

        loop(length - 1, gather_step)
        s_now = w - (length - 1)

        @pl.when((s_now >= 0) & (s_now < chunks))
        def _():
            finish(s_now)

        def reduce_step(k):
            t = length - 2 - k
            s = w - t

            @pl.when((s >= 0) & (s < chunks))
            def _():
                along(s, t)

        loop(length - 1, reduce_step)

    loop(chunks + 2 * length - 2, wave)

    def from_core(s):
        def take(i):
            for yy in range(2):
                gc_copy(s, i, yy, 1 - c).wait_recv()
                use(s, at(i, yy, 1 - c))

        for_z(take)

    def last(s):
        def take(i):
            gy_copy(s, i, 1 - y).wait_recv()
            gc_copy(s, i, 1 - y, c).start()
            use(s, at(i, 1 - y, c))

        for_z(take)

        @pl.when(s > 0)
        def _():
            from_core(s - 1)

    loop(chunks, last)
    from_core(chunks - 1)

    resid_out[...] = 4.0 * (
        labels[...].astype(jnp.float32) - jax.nn.sigmoid(eta[...] + offset_ref[...])
    )

    def drain(s):
        for h in range(2):
            core_copy(s, h).wait_send()
        pair_copy(s).wait_send()

        def step(t):
            for d in range(2):
                place = z if d == 0 else length - 1 - z
                origin = z - t if d == 0 else z + t

                @pl.when((place <= t) & (place < length - 1))
                def _():
                    line_copy(s, t, d).wait_send()

                @pl.when((origin >= 0) & (origin < length) & (place < length - 1))
                def _():
                    gz_copy(s, t, d).wait_send()

        loop(length - 1, step)

        def blocks(i):
            gy_copy(s, i, y).wait_send()
            for yy in range(2):
                gc_copy(s, i, yy, c).wait_send()

        for_z(blocks)

    loop(chunks, drain)


def on_device(genotype, residual, labels, incl_old, mean_old, prior_logit, slab_scale, offset):
    n = lax.axis_size("ind")
    people, _ = genotype.shape
    owned, columns = incl_old.shape
    length = n // 4
    chunks = max(1, min(4, owned // 256))
    rows = owned // chunks
    f32, bf16, i16 = jnp.float32, jnp.bfloat16, jnp.int16
    anywhere = pl.BlockSpec(memory_space=pl.ANY)
    vmem = pl.BlockSpec(memory_space=pltpu.VMEM)
    dma = pltpu.SemaphoreType.DMA
    hops = length - 1
    return pl.pallas_call(
        functools.partial(sweep_kernel, n, chunks),
        out_shape=(
            jax.ShapeDtypeStruct((owned, columns), f32),
            jax.ShapeDtypeStruct((owned, columns), f32),
            jax.ShapeDtypeStruct((people, columns), f32),
        ),
        in_specs=[anywhere, vmem, anywhere, anywhere, anywhere, vmem, vmem, vmem],
        out_specs=(vmem, vmem, vmem),
        scratch_shapes=[
            pltpu.VMEM(genotype.shape, bf16),
            pltpu.VMEM(labels.shape, labels.dtype),
            pltpu.VMEM(incl_old.shape, f32),
            pltpu.VMEM(mean_old.shape, f32),
            pltpu.VMEM((chunks, 2, length, rows, columns), f32),
            pltpu.VMEM((chunks, 2, length, rows, columns), f32),
            pltpu.VMEM((chunks, length, rows, columns), i16),
            pltpu.VMEM((chunks, length, rows, columns), i16),
            pltpu.VMEM((chunks, length, rows, columns), f32),
            pltpu.VMEM((chunks, hops, 2, rows, columns), i16),
            pltpu.VMEM((chunks, hops, 2, rows, columns), i16),
            pltpu.VMEM((chunks, n, rows, columns), bf16),
            pltpu.VMEM((people, columns), f32),
            dma((chunks, n)),
            dma((3,)),
            dma((chunks, 2)),
            dma((chunks, 2)),
            dma((chunks,)),
            dma((chunks,)),
            dma((chunks, hops, 2)),
            dma((chunks, hops, 2)),
            dma((chunks, hops, 2)),
            dma((chunks, hops, 2)),
            dma((chunks, length)),
            dma((chunks, length)),
            dma((chunks, 2, length)),
            dma((chunks, 2, length)),
        ],
        compiler_params=pltpu.CompilerParams(
            collective_id=0, has_side_effects=True, vmem_limit_bytes=67043328
        ),
        name="sweep",
    )(
        genotype, residual, labels, incl_old, mean_old,
        prior_logit.reshape(1, -1), slab_scale.reshape(1, -1), offset.reshape(1, -1),
    )


def solution(mesh):
    placed = (
        P(("groups", "ind"), None),
        P(("groups", "ind"), None),
        P(("groups", "ind"), None),
        P(("groups", "ind"), None),
        P(("groups", "ind"), None),
        P(),
        P(),
        P(),
    )
    return jax.shard_map(
        on_device,
        mesh=mesh,
        in_specs=placed,
        out_specs=(
            P(("groups", "ind"), None),
            P(("groups", "ind"), None),
            P(("groups", "ind"), None),
        ),
        check_vma=False,
    )
```

time: 302 us -> 120 us (0.40)
  waiting for transfers between devices: 253 us -> 0 us
  Pallas kernels: 0 us -> 113 us
  matrix products: 28.5 us -> 0 us
  between operations: 14.1 us -> 0.64 us
  local copies, waits for them, and re-layouts: 2.56 us -> 6.29 us
  other arithmetic: 3.04 us -> 0 us
    reduce_scatter x1 -> x0, waiting for transfers between devices: 180 us -> none  [on_device(): lax.psum_scatter(lax.dot_general(columns, residual, (((0,), (0,)), ((), (...]
    pallas_call x0 -> x1, Pallas kernels: none -> 113 us  [on_device(): pl.pallas_call(functools.partial(sweep_kernel, n, chunks), out_shape=(jax...]
    all_gather x1 -> x0, waiting for transfers between devices: 73.4 us -> none  [on_device(): lax.all_gather(effect, 'ind', axis=0, tiled=True)]
    dot_general x2 -> x0, matrix products: 28.5 us -> none  [the longest x1 14.9 us: on_device(): lax.dot_general(columns, residual, (((0,), (0,)), ((), ())), preferred_el...]
    unnamed x16 -> x3, local copies, waits for them, and re-layouts: 2.56 us -> 6.29 us
    convert_element_type x1 -> x0, other arithmetic: 3.03 us -> none  [update(): effect = (incl_new * mean_new).astype(jnp.bfloat16)]
  transfers between devices with their start and end apart: 2 -> 0, of which waited for: 2 -> 0; matrix products, arithmetic and copies ran while one was open for 0% -> 0% of each run, Pallas kernels for 0% -> 0%
where the time goes in v1:
time: 120 us
  Pallas kernels  113 us (94%)
  local copies, waits for them, and re-layouts  6.29 us (5%)
    pallas_call x1, Pallas kernels, on_device(): pl.pallas_call(functools.partial(sweep_kernel, n, chunks), out_shape=(jax...  113 us
    unnamed x3, local copies, waits for them, and re-layouts  6.29 us

profile of v1, /device:TPU:0, one launch (start us, length us, event | category | flops | bytes accessed | tf_op | source)
XLA Modules:
  0.0 119.8 jit_solution(519361526772904747)
XLA Ops:
  0.6 112.9 %sweep.1 = (f32[1024,256]{1,0:T(8,128)}, f32[1024,256]{1,0:T(8,128)}, f32[384,256]{1,0:T(8,128)}) custom-call(bf16[384,16384]{1,0:T(8,128)(2,1)} %geno_hbm.1, bf16[384,256]{1,0:T(8,128)(2,1)} %resid_ref.1, s32[384,256]{1,0:T(8,128)} %labels_hbm.1, f32[1024,256]{1,0:T(8,128)} %incl_hbm.1, f32[1024,256]{1,0:T(8,128)} %mean_hbm.1, f32[1,256]{1,0:T(1,128)} %bitcast.3, ...), custom_call_target="tpu_custom_call" | custom-call | tf_op jit(solution)/shard_map/sweep/pallas_call | solution.py:344
  113.5 2.3 %copy.14 = f32[1024,256]{1,0:T(8,128)} copy(f32[1024,256]{1,0:T(8,128)} %get-tuple-element.6) | data formatting | bytes 2097152
  115.8 2.3 %copy.15 = f32[1024,256]{1,0:T(8,128)} copy(f32[1024,256]{1,0:T(8,128)} %get-tuple-element.7) | data formatting | bytes 2097152
  118.0 1.8 %copy.16 = f32[384,256]{1,0:T(8,128)} copy(f32[384,256]{1,0:T(8,128)} %get-tuple-element.8) | data formatting | bytes 786432

commit v2 on v1

v2 whole, which is shorter than its diff:
```python
import functools
import math

import jax
import jax.numpy as jnp
from jax import lax
from jax.experimental import pallas as pl
from jax.experimental.pallas import tpu as pltpu
from jax.sharding import PartitionSpec as P

LARGEST_TERM = 64.0


def sweep_kernel(
    n, chunks, period,
    geno_hbm, resid_ref, incl_hbm, mean_hbm, prior_ref, scale_ref,
    stat_out, eta,
    geno, incl, mean, core_out, core_in, pair_out, pair_in, own, line_out, line_in, eff,
    geno_sem, in_sem, core_ss, core_rs, pair_ss, pair_rs, line_ss, line_rs,
    gz_ss, gz_rs, gy_ss, gy_rs, gc_ss, gc_rs,
):
    length = n // 4
    owned = incl.shape[0]
    rows = owned // chunks
    people = geno.shape[0]
    total = float(people * n)
    coding = 32760.0 / math.log(1.0 + LARGEST_TERM * total)
    me = lax.axis_index("ind")
    z = me // 4
    y = (me // 2) % 2
    c = me % 2

    def at(zz, yy, cc):
        return zz * 4 + yy * 2 + cc

    core_dev = {"ind": at(z, y, 1 - c)}
    pair_dev = {"ind": at(z, 1 - y, c)}
    up_dev = {"ind": at(lax.rem(z + 1, length), y, c)}
    down_dev = {"ind": at(lax.rem(z + length - 1, length), y, c)}
    has_up = z < length - 1
    has_down = z > 0

    def remote(src, dst, ss, rs, dev):
        return pltpu.make_async_remote_copy(
            src_ref=src, dst_ref=dst, send_sem=ss, recv_sem=rs,
            device_id=dev, device_id_type=pl.DeviceIdType.MESH,
        )

    def encode(x):
        code = (jnp.log(1.0 + jnp.abs(x)) * coding + 0.5).astype(jnp.int32)
        return jnp.where(x < 0.0, -code, code).astype(jnp.int16)

    def decode(code):
        level = code.astype(jnp.int32).astype(jnp.float32)
        size = jnp.exp(jnp.abs(level) * (1.0 / coding)) - 1.0
        return jnp.where(level < 0.0, -size, size)

    def cols(s, o):
        return pl.ds(pl.multiple_of(o * owned + s * rows, 128), rows)

    def load(s, o):
        return pltpu.make_async_copy(
            geno_hbm.at[:, cols(s, o)], geno.at[:, cols(s, o)], geno_sem.at[s, o]
        )

    def for_z(body):
        lax.fori_loop(0, length, lambda i, _: (body(i), 0)[1], 0)

    def loop(count, body):
        lax.fori_loop(0, count, lambda i, _: (body(i), 0)[1], 0)

    owners = ((1 - y, 1 - c), (y, 1 - c), (y, c), (1 - y, c))

    def load_chunk(s):
        for yy, cc in owners:
            for_z(lambda i: load(s, at(i, yy, cc)).start())

    loop(chunks, load_chunk)
    small = [
        pltpu.make_async_copy(incl_hbm, incl, in_sem.at[0]),
        pltpu.make_async_copy(mean_hbm, mean, in_sem.at[1]),
    ]
    for copy in small:
        copy.start()

    barrier = pltpu.get_barrier_semaphore()
    pl.semaphore_signal(barrier, inc=1, device_id=core_dev, device_id_type=pl.DeviceIdType.MESH)
    pl.semaphore_signal(barrier, inc=1, device_id=pair_dev, device_id_type=pl.DeviceIdType.MESH)

    @pl.when(has_up)
    def _():
        pl.semaphore_signal(barrier, inc=1, device_id=up_dev, device_id_type=pl.DeviceIdType.MESH)

    @pl.when(has_down)
    def _():
        pl.semaphore_signal(barrier, inc=1, device_id=down_dev, device_id_type=pl.DeviceIdType.MESH)

    pl.semaphore_wait(barrier, 2 + has_up.astype(jnp.int32) + has_down.astype(jnp.int32))

    def product(s, o):
        load(s, o).wait()
        return lax.dot_general(
            geno[:, cols(s, o)], resid_ref[...], (((0,), (0,)), ((), ())),
            preferred_element_type=jnp.float32,
        )

    def line_first(s):
        return lax.rem(s, period) == 0 if period else s < 0

    def flows(s):
        return 1 + line_first(s).astype(jnp.int32) if period else 1

    def slot(s, f):
        if not period:
            return s
        k = lax.rem(s, period)
        return (s // period) * (period + 1) + k + jnp.where(k == 0, f, 1)

    def side(f):
        return jnp.where(f == 0, y, 1 - y)

    def core_copy(s, h):
        return remote(
            core_out.at[s % 2, h], core_in.at[s, h], core_ss.at[s, h], core_rs.at[s, h], core_dev
        )

    def pair_copy(s):
        return remote(pair_out.at[s], pair_in.at[s], pair_ss.at[s], pair_rs.at[s], pair_dev)

    def pair_one(s):
        return remote(
            pair_out.at[s, 0], pair_in.at[s, 0], pair_ss.at[s], pair_rs.at[s], pair_dev
        )

    def line_copy(s, t, d, f):
        k = slot(s, f)
        return remote(
            line_out.at[k, t, d], line_in.at[k, t, d], line_ss.at[k, t, d], line_rs.at[k, t, d],
            up_dev if d == 0 else down_dev,
        )

    def first(s):
        for h in range(2):
            yy, cc = owners[h]

            @pl.when(s >= 2)
            def _():
                core_copy(s - 2, h).wait_send()

            def part(i):
                core_out[s % 2, h, i] = product(s, at(i, yy, cc))

            for_z(part)
            core_copy(s, h).start()

        def keep(i):
            own[slot(s, 0), i] = product(s, at(i, y, c))

        for_z(keep)

        @pl.when(line_first(s))
        def _():
            def keep_other(i):
                own[slot(s, 1), i] = product(s, at(i, 1 - y, c))

            for_z(keep_other)

        @pl.when(jnp.logical_not(line_first(s)))
        def _():
            core_copy(s, 0).wait_recv()

            def pass_on(i):
                pair_out[s, i] = encode(product(s, at(i, 1 - y, c)) + core_in[s, 0, i])

            for_z(pass_on)
            pair_copy(s).start()

    loop(chunks, first)
    for copy in small:
        copy.wait()
    eta[...] = jnp.zeros_like(eta)

    scale = scale_ref[...]
    shrink = scale / (1.0 + scale)
    bias = prior_ref[...] - 0.5 * jnp.log1p(scale)
    curve = 0.5 * total * shrink

    def settle(s):
        core_copy(s, 1).wait_recv()

        @pl.when(line_first(s))
        def _():
            core_copy(s, 0).wait_recv()

            def add(i):
                for f in range(2):
                    k = slot(s, f)
                    own[k, i] = own[k, i] + core_in[s, 1 - f, i]

            for_z(add)

        @pl.when(jnp.logical_not(line_first(s)))
        def _():
            pair_copy(s).wait_recv()

            def add(i):
                k = slot(s, 0)
                own[k, i] = own[k, i] + core_in[s, 1, i] + decode(pair_in[s, i])

            for_z(add)

    def along(s, t):
        @pl.when(t == 0)
        def _():
            settle(s)

        def flow(f):
            k = slot(s, f)
            for d in range(2):
                place = z if d == 0 else length - 1 - z
                block = length - 1 - t + z if d == 0 else t - (length - 1 - z)

                @pl.when((place <= t) & (place < length - 1))
                def _():
                    @pl.when(place == 0)
                    def _():
                        line_out[k, t, d] = encode(own[k, block])

                    @pl.when(place > 0)
                    def _():
                        line_copy(s, t - 1, d, f).wait_recv()
                        line_out[k, t, d] = encode(own[k, block] + decode(line_in[k, t - 1, d]))

                    line_copy(s, t, d, f).start()

        loop(flows(s), flow)

    def gz_copy(s, u, d, f):
        k, o = slot(s, f), at(z - u if d == 0 else z + u, side(f), c)
        return remote(
            eff.at[s, o], eff.at[s, o], gz_ss.at[k, u, d], gz_rs.at[k, u, d], up_dev if d == 0 else down_dev
        )

    def gz_landed(s, u, d, f):
        k, o = slot(s, f), at(z - 1 - u if d == 0 else z + 1 + u, side(f), c)
        return remote(
            eff.at[s, o], eff.at[s, o], gz_ss.at[k, u, d], gz_rs.at[k, u, d], up_dev if d == 0 else down_dev
        )

    def gy_copy(s, i, yy):
        o = at(i, yy, c)
        return remote(eff.at[s, o], eff.at[s, o], gy_ss.at[s, i], gy_rs.at[s, i], pair_dev)

    def gc_copy(s, i, yy, cc):
        o = at(i, yy, cc)
        return remote(eff.at[s, o], eff.at[s, o], gc_ss.at[s, yy, i], gc_rs.at[s, yy, i], core_dev)

    def use(s, o):
        eta[...] += jnp.dot(geno[:, cols(s, o)], eff[s, o], preferred_element_type=jnp.float32)

    def send_own(s, f):
        @pl.when(has_up)
        def _():
            gz_copy(s, 0, 0, f).start()

        @pl.when(has_down)
        def _():
            gz_copy(s, 0, 1, f).start()

        gc_copy(s, z, side(f), c).start()

    def total_of_line(s):
        def flow(f):
            k = slot(s, f)
            for d in range(2):
                @pl.when(has_down if d == 0 else has_up)
                def _():
                    line_copy(s, length - 2, d, f).wait_recv()
                    own[k, z] = own[k, z] + decode(line_in[k, length - 2, d])

        loop(flows(s), flow)

        @pl.when(line_first(s))
        def _():
            pair_out[s, 0] = encode(own[slot(s, 1), z])
            pair_one(s).start()

        @pl.when(jnp.logical_not(line_first(s)))
        def _():
            finish(s)

    def total_of_pair(s):
        pair_one(s).wait_recv()
        own[slot(s, 0), z] = own[slot(s, 0), z] + decode(pair_in[s, 0])
        finish(s)

    def finish(s):
        here = pl.ds(pl.multiple_of(s * rows, 8), rows)
        before = incl[here, :]
        stat = own[slot(s, 0), z] / total + before * mean[here, :]
        stat_out[here, :] = stat
        incl_new = 0.5 * before + 0.5 * jax.nn.sigmoid(bias + curve * stat * stat)
        eff[s, me] = (incl_new * (stat * shrink)).astype(jnp.bfloat16)
        gy_copy(s, z, y).start()
        send_own(s, 0)
        use(s, me)

    def send_other(s):
        gy_copy(s, z, 1 - y).wait_recv()
        send_own(s, 1)
        use(s, at(z, 1 - y, c))

    def spread(s, u, f):
        for d in range(2):
            source = z - u if d == 0 else z + u

            @pl.when((source >= 0) & (source < length))
            def _():
                gz_landed(s, u - 1, d, f).wait_recv()

                @pl.when(has_up if d == 0 else has_down)
                def _():
                    gz_copy(s, u, d, f).start()

                @pl.when(jnp.logical_not(line_first(s)))
                def _():
                    gy_copy(s, source, y).start()

                gc_copy(s, source, side(f), c).start()
                use(s, at(source, side(f), c))

    def within(s):
        return (s >= 0) & (s < chunks)

    def wave(w):
        def gather_step(k):
            u = length - 1 - k
            kinds = [(w - (length - 1) - u, 0, False)]
            if period:
                kinds = [(w - length - 1 - u, 1, True), (w - length - u, 0, True)] + kinds
            for s, f, kind in kinds:
                @pl.when(within(s) & (line_first(s) if kind else jnp.logical_not(line_first(s))))
                def _():
                    spread(s, u, f)

        loop(length - 1, gather_step)
        if period:
            @pl.when(within(w - length - 1) & line_first(w - length - 1))
            def _():
                send_other(w - length - 1)

            @pl.when(within(w - length) & line_first(w - length))
            def _():
                total_of_pair(w - length)

        @pl.when(within(w - (length - 1)))
        def _():
            total_of_line(w - (length - 1))

        def reduce_step(k):
            t = length - 2 - k

            @pl.when(within(w - t))
            def _():
                along(w - t, t)

        loop(length - 1, reduce_step)

    loop(chunks + 2 * length, wave)

    def from_core(s):
        def take(i):
            for yy in range(2):
                gc_copy(s, i, yy, 1 - c).wait_recv()
                use(s, at(i, yy, 1 - c))

        for_z(take)

    def last(s):
        def take(i):
            gy_copy(s, i, 1 - y).wait_recv()
            gc_copy(s, i, 1 - y, c).start()
            use(s, at(i, 1 - y, c))

        @pl.when(jnp.logical_not(line_first(s)))
        def _():
            for_z(take)

        @pl.when(s > 0)
        def _():
            from_core(s - 1)

    loop(chunks, last)
    from_core(chunks - 1)

    def drain(s):
        @pl.when(s >= chunks - 2)
        def _():
            for h in range(2):
                core_copy(s, h).wait_send()

        @pl.when(line_first(s))
        def _():
            pair_one(s).wait_send()
            gy_copy(s, z, y).wait_send()

        @pl.when(jnp.logical_not(line_first(s)))
        def _():
            pair_copy(s).wait_send()
            for_z(lambda i: gy_copy(s, i, y).wait_send())

        def flow(f):
            def step(t):
                for d in range(2):
                    place = z if d == 0 else length - 1 - z
                    origin = z - t if d == 0 else z + t

                    @pl.when((place <= t) & (place < length - 1))
                    def _():
                        line_copy(s, t, d, f).wait_send()

                    @pl.when((origin >= 0) & (origin < length) & (place < length - 1))
                    def _():
                        gz_copy(s, t, d, f).wait_send()

            loop(length - 1, step)

        loop(flows(s), flow)

        def blocks(i):
            for yy in range(2):
                gc_copy(s, i, yy, c).wait_send()

        for_z(blocks)

    loop(chunks, drain)


def outputs_kernel(
    half_total, stat_ref, incl_ref, eta_ref, labels_ref, prior_ref, scale_ref, offset_ref,
    incl_out, mean_out, resid_out,
):
    scale = scale_ref[...]
    shrink = scale / (1.0 + scale)
    bias = prior_ref[...] - 0.5 * jnp.log1p(scale)
    stat = stat_ref[...]
    mean_out[...] = stat * shrink
    logit = bias + (half_total * shrink) * stat * stat
    incl_out[...] = 0.5 * incl_ref[...] + 0.5 * jax.nn.sigmoid(logit)
    resid_out[...] = 4.0 * (
        labels_ref[...].astype(jnp.float32) - jax.nn.sigmoid(eta_ref[...] + offset_ref[...])
    )


def on_device(genotype, residual, labels, incl_old, mean_old, prior_logit, slab_scale, offset):
    n = lax.axis_size("ind")
    people, _ = genotype.shape
    owned, columns = incl_old.shape
    length = n // 4
    chunks = max(1, min(4, owned // 256))
    period = 2 if chunks % 2 == 0 else 0
    slots = chunks + chunks // 2 if period else chunks
    rows = owned // chunks
    f32, bf16, i16 = jnp.float32, jnp.bfloat16, jnp.int16
    anywhere = pl.BlockSpec(memory_space=pl.ANY)
    vmem = pl.BlockSpec(memory_space=pltpu.VMEM)
    dma = pltpu.SemaphoreType.DMA
    hops = length - 1
    prior, scale, shift = (v.reshape(1, -1) for v in (prior_logit, slab_scale, offset))
    stat, eta = pl.pallas_call(
        functools.partial(sweep_kernel, n, chunks, period),
        out_shape=(
            jax.ShapeDtypeStruct((owned, columns), f32),
            jax.ShapeDtypeStruct((people, columns), f32),
        ),
        in_specs=[anywhere, vmem, anywhere, anywhere, vmem, vmem],
        out_specs=(vmem, vmem),
        scratch_shapes=[
            pltpu.VMEM(genotype.shape, bf16),
            pltpu.VMEM(incl_old.shape, f32),
            pltpu.VMEM(mean_old.shape, f32),
            pltpu.VMEM((min(chunks, 2), 2, length, rows, columns), f32),
            pltpu.VMEM((chunks, 2, length, rows, columns), f32),
            pltpu.VMEM((chunks, length, rows, columns), i16),
            pltpu.VMEM((chunks, length, rows, columns), i16),
            pltpu.VMEM((slots, length, rows, columns), f32),
            pltpu.VMEM((slots, hops, 2, rows, columns), i16),
            pltpu.VMEM((slots, hops, 2, rows, columns), i16),
            pltpu.VMEM((chunks, n, rows, columns), bf16),
            dma((chunks, n)),
            dma((2,)),
            dma((chunks, 2)),
            dma((chunks, 2)),
            dma((chunks,)),
            dma((chunks,)),
            dma((slots, hops, 2)),
            dma((slots, hops, 2)),
            dma((slots, hops, 2)),
            dma((slots, hops, 2)),
            dma((chunks, length)),
            dma((chunks, length)),
            dma((chunks, 2, length)),
            dma((chunks, 2, length)),
        ],
        compiler_params=pltpu.CompilerParams(
            collective_id=0, has_side_effects=True, vmem_limit_bytes=67043328
        ),
        name="sweep",
    )(genotype, residual, incl_old, mean_old, prior, scale)

    steps = 4 if owned % 32 == 0 and people % 32 == 0 else 1
    upper = pl.BlockSpec((owned // steps, columns), lambda i: (i, 0))
    lower = pl.BlockSpec((people // steps, columns), lambda i: (i, 0))
    flat = pl.BlockSpec((1, columns), lambda i: (0, 0))
    return pl.pallas_call(
        functools.partial(outputs_kernel, 0.5 * people * n),
        grid=(steps,),
        out_shape=(
            jax.ShapeDtypeStruct((owned, columns), f32),
            jax.ShapeDtypeStruct((owned, columns), f32),
            jax.ShapeDtypeStruct((people, columns), f32),
        ),
        in_specs=[upper, upper, lower, lower, flat, flat, flat],
        out_specs=(upper, upper, lower),
        name="outputs",
    )(stat, incl_old, eta, labels, prior, scale, shift)


def solution(mesh):
    placed = (
        P(("groups", "ind"), None),
        P(("groups", "ind"), None),
        P(("groups", "ind"), None),
        P(("groups", "ind"), None),
        P(("groups", "ind"), None),
        P(),
        P(),
        P(),
    )
    return jax.shard_map(
        on_device,
        mesh=mesh,
        in_specs=placed,
        out_specs=(
            P(("groups", "ind"), None),
            P(("groups", "ind"), None),
            P(("groups", "ind"), None),
        ),
        check_vma=False,
    )
```

time: 120 us -> 140 us (1.17)
  Pallas kernels: 113 us -> 139 us
  local copies, waits for them, and re-layouts: 6.29 us -> 0 us
    pallas_call x1 -> x2, Pallas kernels: 113 us -> 139 us  [the longest x1 135 us: on_device(): pl.pallas_call(functools.partial(sweep_kernel, n, chunks, period), out_sh...]
    unnamed x3 -> x0, local copies, waits for them, and re-layouts: 6.29 us -> none
where the time goes in v2:
time: 140 us
  Pallas kernels  139 us (99%)
    pallas_call x1, Pallas kernels, on_device(): pl.pallas_call(functools.partial(sweep_kernel, n, chunks, period), out_sh...  135 us
    pallas_call x1, Pallas kernels, on_device(): pl.pallas_call(functools.partial(outputs_kernel, 0.5 * people * n), grid=...  3.95 us

profile of v2, /device:TPU:0, one launch (start us, length us, event | category | flops | bytes accessed | tf_op | source)
XLA Modules:
  0.0 139.6 jit_solution(16967708963839477731)
XLA Ops:
  0.6 135.0 %sweep.1 = (f32[1024,256]{1,0:T(8,128)}, f32[384,256]{1,0:T(8,128)}) custom-call(bf16[384,16384]{1,0:T(8,128)(2,1)} %geno_hbm.1, bf16[384,256]{1,0:T(8,128)(2,1)} %resid_ref.1, f32[1024,256]{1,0:T(8,128)} %incl_ref.1, f32[1024,256]{1,0:T(8,128)} %mean_hbm.1, f32[1,256]{1,0:T(1,128)} %bitcast.3, f32[1,256]{1,0:T(1,128)} %bitcast.5), custom_call_target="tpu_custom_call" | custom-call | tf_op jit(solution)/shard_map/sweep/pallas_call | solution.py:470
  135.6 4.0 %outputs.1 = (f32[1024,256]{1,0:T(8,128)}, f32[1024,256]{1,0:T(8,128)}, f32[384,256]{1,0:T(8,128)}) custom-call(f32[1024,256]{1,0:T(8,128)} %get-tuple-element.5.stat_ref, f32[1024,256]{1,0:T(8,128)} %incl_ref.1, f32[384,256]{1,0:T(8,128)} %get-tuple-element.6.eta_ref, s32[384,256]{1,0:T(8,128)} %labels_ref.1, f32[1,256]{1,0:T(1,128)} %bitcast.4, ...), custom_call_target="tpu_custom_call" | custom-call | tf_op jit(solution)/shard_map/outputs/pallas_call | solution.py:515

commit v3 on v1

--- a/solution.py
+++ b/solution.py
@@ -12,10 +12,10 @@
 
 
 def sweep_kernel(
-    n, chunks,
-    geno_hbm, resid_ref, labels_hbm, incl_hbm, mean_hbm, prior_ref, scale_ref, offset_ref,
-    incl_out, mean_out, resid_out,
-    geno, labels, incl, mean, core_out, core_in, pair_out, pair_in, own, line_out, line_in, eff, eta,
+    n, chunks, wide_chunks,
+    geno_hbm, resid_ref, incl_hbm, mean_hbm, prior_ref, scale_ref,
+    stat_out, eta,
+    geno, incl, mean, core_out, core_in, pair_out, pair_in, own, line_out, line_in, eff,
     geno_sem, in_sem, core_ss, core_rs, pair_ss, pair_rs, line_ss, line_rs,
     gz_ss, gz_rs, gy_ss, gy_rs, gc_ss, gc_rs,
 ):
@@ -77,9 +77,8 @@
 
     loop(chunks, load_chunk)
     small = [
-        pltpu.make_async_copy(labels_hbm, labels, in_sem.at[0]),
-        pltpu.make_async_copy(incl_hbm, incl, in_sem.at[1]),
-        pltpu.make_async_copy(mean_hbm, mean, in_sem.at[2]),
+        pltpu.make_async_copy(incl_hbm, incl, in_sem.at[0]),
+        pltpu.make_async_copy(mean_hbm, mean, in_sem.at[1]),
     ]
     for copy in small:
         copy.start()
@@ -105,8 +104,16 @@
             preferred_element_type=jnp.float32,
         )
 
+    def wide(s):
+        return s >= chunks - wide_chunks
+
+    def side(f):
+        return jnp.where(f == 0, y, 1 - y)
+
     def core_copy(s, h):
-        return remote(core_out.at[s, h], core_in.at[s, h], core_ss.at[s, h], core_rs.at[s, h], core_dev)
+        return remote(
+            core_out.at[s % 2, h], core_in.at[s, h], core_ss.at[s, h], core_rs.at[s, h], core_dev
+        )
 
     def pair_copy(s):
         return remote(pair_out.at[s], pair_in.at[s], pair_ss.at[s], pair_rs.at[s], pair_dev)
@@ -118,15 +125,21 @@
         )
 
     def first(s):
-        for h in range(2):
+        def to_core(h):
             yy, cc = owners[h]
 
+            @pl.when(s >= 2)
+            def _():
+                core_copy(s - 2, h).wait_send()
+
             def part(i):
-                core_out[s, h, i] = product(s, at(i, yy, cc))
+                core_out[s % 2, h, i] = product(s, at(i, yy, cc))
 
             for_z(part)
             core_copy(s, h).start()
 
+        to_core(0)
+
         def keep(i):
             own[s, i] = product(s, at(i, y, c))
 
@@ -138,6 +151,7 @@
 
         for_z(pass_on)
         pair_copy(s).start()
+        to_core(1)
 
     loop(chunks, first)
     for copy in small:
@@ -177,16 +191,16 @@
 
                 line_copy(s, t, d).start()
 
-    def gz_copy(s, u, d):
-        o = at(z - u if d == 0 else z + u, y, c)
+    def gz_copy(s, u, d, f):
+        k, o = 2 * s + f, at(z - u if d == 0 else z + u, side(f), c)
         return remote(
-            eff.at[s, o], eff.at[s, o], gz_ss.at[s, u, d], gz_rs.at[s, u, d], up_dev if d == 0 else down_dev
-        )
-
-    def gz_landed(s, u, d):
-        o = at(z - 1 - u if d == 0 else z + 1 + u, y, c)
+            eff.at[s, o], eff.at[s, o], gz_ss.at[k, u, d], gz_rs.at[k, u, d], up_dev if d == 0 else down_dev
+        )
+
+    def gz_landed(s, u, d, f):
+        k, o = 2 * s + f, at(z - 1 - u if d == 0 else z + 1 + u, side(f), c)
         return remote(
-            eff.at[s, o], eff.at[s, o], gz_ss.at[s, u, d], gz_rs.at[s, u, d], up_dev if d == 0 else down_dev
+            eff.at[s, o], eff.at[s, o], gz_ss.at[k, u, d], gz_rs.at[k, u, d], up_dev if d == 0 else down_dev
         )
 
     def gy_copy(s, i, yy):
@@ -200,6 +214,17 @@
     def use(s, o):
         eta[...] += jnp.dot(geno[:, cols(s, o)], eff[s, o], preferred_element_type=jnp.float32)
 
+    def send_own(s, f):
+        @pl.when(has_up)
+        def _():
+            gz_copy(s, 0, 0, f).start()
+
+        @pl.when(has_down)
+        def _():
+            gz_copy(s, 0, 1, f).start()
+
+        gc_copy(s, z, side(f), c).start()
+
     def finish(s):
         for d in range(2):
             @pl.when(has_down if d == 0 else has_up)
@@ -210,67 +235,39 @@
         here = pl.ds(pl.multiple_of(s * rows, 8), rows)
         before = incl[here, :]
         stat = own[s, z] / total + before * mean[here, :]
-        mean_new = stat * shrink
+        stat_out[here, :] = stat
         incl_new = 0.5 * before + 0.5 * jax.nn.sigmoid(bias + curve * stat * stat)
-        mean_out[here, :] = mean_new
-        incl_out[here, :] = incl_new
-        eff[s, me] = (incl_new * mean_new).astype(jnp.bfloat16)
-
-        @pl.when(has_up)
-        def _():
-            gz_copy(s, 0, 0).start()
-
-        @pl.when(has_down)
-        def _():
-            gz_copy(s, 0, 1).start()
-
+        eff[s, me] = (incl_new * (stat * shrink)).astype(jnp.bfloat16)
         gy_copy(s, z, y).start()
-        gc_copy(s, z, y, c).start()
+        send_own(s, 0)
         use(s, me)
 
-    def spread(s, u):
+    def send_other(s):
+        gy_copy(s, z, 1 - y).wait_recv()
+        send_own(s, 1)
+        use(s, at(z, 1 - y, c))
+
+    def spread(s, u, f):
         for d in range(2):
             source = z - u if d == 0 else z + u
 
             @pl.when((source >= 0) & (source < length))
             def _():
-                gz_landed(s, u - 1, d).wait_recv()
+                gz_landed(s, u - 1, d, f).wait_recv()
 
                 @pl.when(has_up if d == 0 else has_down)
                 def _():
-                    gz_copy(s, u, d).start()
-
-                gy_copy(s, source, y).start()
-                gc_copy(s, source, y, c).start()
-                use(s, at(source, y, c))
-
-    def wave(w):
-        def gather_step(k):
-            u = length - 1 - k
-            s = w - (length - 1) - u
-
-            @pl.when((s >= 0) & (s < chunks))
-            def _():
-                spread(s, u)
-
-        loop(length - 1, gather_step)
-        s_now = w - (length - 1)
-
-        @pl.when((s_now >= 0) & (s_now < chunks))
-        def _():
-            finish(s_now)
-
-        def reduce_step(k):
-            t = length - 2 - k
-            s = w - t
-
-            @pl.when((s >= 0) & (s < chunks))
-            def _():
-                along(s, t)
-
-        loop(length - 1, reduce_step)
-
-    loop(chunks + 2 * length - 2, wave)
+                    gz_copy(s, u, d, f).start()
+
+                @pl.when(jnp.logical_not(wide(s)))
+                def _():
+                    gy_copy(s, source, y).start()
+
+                gc_copy(s, source, side(f), c).start()
+                use(s, at(source, side(f), c))
+
+    def within(s):
+        return (s >= 0) & (s < chunks)
 
     def from_core(s):
         def take(i):
@@ -286,23 +283,71 @@
             gc_copy(s, i, 1 - y, c).start()
             use(s, at(i, 1 - y, c))
 
-        for_z(take)
+        @pl.when(jnp.logical_not(wide(s)))
+        def _():
+            for_z(take)
 
         @pl.when(s > 0)
         def _():
             from_core(s - 1)
 
-    loop(chunks, last)
+    def wave(w):
+        def gather_step(k):
+            u = length - 1 - k
+            s = w - (length - 1) - u
+
+            @pl.when(within(s - 1) & wide(s - 1))
+            def _():
+                spread(s - 1, u, 1)
+
+            @pl.when(within(s))
+            def _():
+                spread(s, u, 0)
+
+        loop(length - 1, gather_step)
+        here = w - (length - 1)
+
+        @pl.when(within(here - 1) & wide(here - 1))
+        def _():
+            send_other(here - 1)
+
+        @pl.when(within(here))
+        def _():
+            finish(here)
+
+        def reduce_step(k):
+            t = length - 2 - k
+
+            @pl.when(within(w - t))
+            def _():
+                along(w - t, t)
+
+        loop(length - 1, reduce_step)
+
+        @pl.when(within(w - 2 * length + 1))
+        def _():
+            last(w - 2 * length + 1)
+
+    loop(chunks + 2 * length - 1, wave)
     from_core(chunks - 1)
 
-    resid_out[...] = 4.0 * (
-        labels[...].astype(jnp.float32) - jax.nn.sigmoid(eta[...] + offset_ref[...])
-    )
-
     def drain(s):
-        for h in range(2):
-            core_copy(s, h).wait_send()
+        @pl.when(s >= chunks - 2)
+        def _():
+            for h in range(2):
+                core_copy(s, h).wait_send()
+
         pair_copy(s).wait_send()
+        gy_copy(s, z, y).wait_send()
+
+        @pl.when(jnp.logical_not(wide(s)))
+        def _():
+            def sent(i):
+                @pl.when(i != z)
+                def _():
+                    gy_copy(s, i, y).wait_send()
+
+            for_z(sent)
 
         def step(t):
             for d in range(2):
@@ -315,18 +360,37 @@
 
                 @pl.when((origin >= 0) & (origin < length) & (place < length - 1))
                 def _():
-                    gz_copy(s, t, d).wait_send()
+                    gz_copy(s, t, d, 0).wait_send()
+
+                    @pl.when(wide(s))
+                    def _():
+                        gz_copy(s, t, d, 1).wait_send()
 
         loop(length - 1, step)
 
         def blocks(i):
-            gy_copy(s, i, y).wait_send()
             for yy in range(2):
                 gc_copy(s, i, yy, c).wait_send()
 
         for_z(blocks)
 
     loop(chunks, drain)
+
+
+def outputs_kernel(
+    half_total, stat_ref, incl_ref, eta_ref, labels_ref, prior_ref, scale_ref, offset_ref,
+    incl_out, mean_out, resid_out,
+):
+    scale = scale_ref[...]
+    shrink = scale / (1.0 + scale)
+    bias = prior_ref[...] - 0.5 * jnp.log1p(scale)
+    stat = stat_ref[...]
+    mean_out[...] = stat * shrink
+    logit = bias + (half_total * shrink) * stat * stat
+    incl_out[...] = 0.5 * incl_ref[...] + 0.5 * jax.nn.sigmoid(logit)
+    resid_out[...] = 4.0 * (
+        labels_ref[...].astype(jnp.float32) - jax.nn.sigmoid(eta_ref[...] + offset_ref[...])
+    )
 
 
 def on_device(genotype, residual, labels, incl_old, mean_old, prior_logit, slab_scale, offset):
@@ -335,27 +399,27 @@
     owned, columns = incl_old.shape
     length = n // 4
     chunks = max(1, min(4, owned // 256))
+    wide_chunks = 0
     rows = owned // chunks
     f32, bf16, i16 = jnp.float32, jnp.bfloat16, jnp.int16
     anywhere = pl.BlockSpec(memory_space=pl.ANY)
     vmem = pl.BlockSpec(memory_space=pltpu.VMEM)
     dma = pltpu.SemaphoreType.DMA
     hops = length - 1
-    return pl.pallas_call(
-        functools.partial(sweep_kernel, n, chunks),
+    prior, scale, shift = (v.reshape(1, -1) for v in (prior_logit, slab_scale, offset))
+    stat, eta = pl.pallas_call(
+        functools.partial(sweep_kernel, n, chunks, wide_chunks),
         out_shape=(
-            jax.ShapeDtypeStruct((owned, columns), f32),
             jax.ShapeDtypeStruct((owned, columns), f32),
             jax.ShapeDtypeStruct((people, columns), f32),
         ),
-        in_specs=[anywhere, vmem, anywhere, anywhere, anywhere, vmem, vmem, vmem],
-        out_specs=(vmem, vmem, vmem),
+        in_specs=[anywhere, vmem, anywhere, anywhere, vmem, vmem],
+        out_specs=(vmem, vmem),
         scratch_shapes=[
             pltpu.VMEM(genotype.shape, bf16),
-            pltpu.VMEM(labels.shape, labels.dtype),
             pltpu.VMEM(incl_old.shape, f32),
             pltpu.VMEM(mean_old.shape, f32),
-            pltpu.VMEM((chunks, 2, length, rows, columns), f32),
+            pltpu.VMEM((min(chunks, 2), 2, length, rows, columns), f32),
             pltpu.VMEM((chunks, 2, length, rows, columns), f32),
             pltpu.VMEM((chunks, length, rows, columns), i16),
             pltpu.VMEM((chunks, length, rows, columns), i16),
@@ -363,17 +427,16 @@
             pltpu.VMEM((chunks, hops, 2, rows, columns), i16),
             pltpu.VMEM((chunks, hops, 2, rows, columns), i16),
             pltpu.VMEM((chunks, n, rows, columns), bf16),
-            pltpu.VMEM((people, columns), f32),
             dma((chunks, n)),
-            dma((3,)),
+            dma((2,)),
             dma((chunks, 2)),
             dma((chunks, 2)),
             dma((chunks,)),
             dma((chunks,)),
             dma((chunks, hops, 2)),
             dma((chunks, hops, 2)),
-            dma((chunks, hops, 2)),
-            dma((chunks, hops, 2)),
+            dma((2 * chunks, hops, 2)),
+            dma((2 * chunks, hops, 2)),
             dma((chunks, length)),
             dma((chunks, length)),
             dma((chunks, 2, length)),
@@ -383,10 +446,24 @@
             collective_id=0, has_side_effects=True, vmem_limit_bytes=67043328
         ),
         name="sweep",
-    )(
-        genotype, residual, labels, incl_old, mean_old,
-        prior_logit.reshape(1, -1), slab_scale.reshape(1, -1), offset.reshape(1, -1),
-    )
+    )(genotype, residual, incl_old, mean_old, prior, scale)
+
+    steps = 4 if owned % 32 == 0 and people % 32 == 0 else 1
+    upper = pl.BlockSpec((owned // steps, columns), lambda i: (i, 0))
+    lower = pl.BlockSpec((people // steps, columns), lambda i: (i, 0))
+    flat = pl.BlockSpec((1, columns), lambda i: (0, 0))
+    return pl.pallas_call(
+        functools.partial(outputs_kernel, 0.5 * people * n),
+        grid=(steps,),
+        out_shape=(
+            jax.ShapeDtypeStruct((owned, columns), f32),
+            jax.ShapeDtypeStruct((owned, columns), f32),
+            jax.ShapeDtypeStruct((people, columns), f32),
+        ),
+        in_specs=[upper, upper, lower, lower, flat, flat, flat],
+        out_specs=(upper, upper, lower),
+        name="outputs",
+    )(stat, incl_old, eta, labels, prior, scale, shift)
 
 
 def solution(mesh):

time: 120 us -> 115 us (0.958)
  local copies, waits for them, and re-layouts: 6.29 us -> 0 us
    unnamed x3 -> x0, local copies, waits for them, and re-layouts: 6.29 us -> none
    pallas_call x1 -> x2, Pallas kernels: 113 us -> 114 us  [the longest x1 110 us: on_device(): pl.pallas_call(functools.partial(sweep_kernel, n, chunks, wide_chunks), o...]
where the time goes in v3:
time: 115 us
  Pallas kernels  114 us (99%)
    pallas_call x1, Pallas kernels, on_device(): pl.pallas_call(functools.partial(sweep_kernel, n, chunks, wide_chunks), o...  110 us
    pallas_call x1, Pallas kernels, on_device(): pl.pallas_call(functools.partial(outputs_kernel, 0.5 * people * n), grid=...  3.95 us

profile of v3, /device:TPU:0, one launch (start us, length us, event | category | flops | bytes accessed | tf_op | source)
XLA Modules:
  0.0 115.0 jit_solution(4654424786767720904)
XLA Ops:
  0.6 110.4 %sweep.1 = (f32[1024,256]{1,0:T(8,128)}, f32[384,256]{1,0:T(8,128)}) custom-call(bf16[384,16384]{1,0:T(8,128)(2,1)} %geno_hbm.1, bf16[384,256]{1,0:T(8,128)(2,1)} %resid_ref.1, f32[1024,256]{1,0:T(8,128)} %incl_ref.1, f32[1024,256]{1,0:T(8,128)} %mean_hbm.1, f32[1,256]{1,0:T(1,128)} %bitcast.3, f32[1,256]{1,0:T(1,128)} %bitcast.5), custom_call_target="tpu_custom_call" | custom-call | tf_op jit(solution)/shard_map/sweep/pallas_call | solution.py:410
  111.1 4.0 %outputs.1 = (f32[1024,256]{1,0:T(8,128)}, f32[1024,256]{1,0:T(8,128)}, f32[384,256]{1,0:T(8,128)}) custom-call(f32[1024,256]{1,0:T(8,128)} %get-tuple-element.5.stat_ref, f32[1024,256]{1,0:T(8,128)} %incl_ref.1, f32[384,256]{1,0:T(8,128)} %get-tuple-element.6.eta_ref, s32[384,256]{1,0:T(8,128)} %labels_ref.1, f32[1,256]{1,0:T(1,128)} %bitcast.4, ...), custom_call_target="tpu_custom_call" | custom-call | tf_op jit(solution)/shard_map/outputs/pallas_call | solution.py:455
